TPU v7x, 128 devices: a whole 4x4x4 slice. The times are simulated.
128 devices in a mesh: fsdp: 32 (over x, z, core), tensor: 4 (over y).
Axes of the slice: x: 4, y: 4, z: 4, core: 2. Of those that a mesh axis runs over, the one named last changes fastest.
Arguments:
- tokens: bfloat16 [24576, 8192], P('fsdp'), may hold values from -6 to 6
- weight: bfloat16 [8192, 8192], P('fsdp', 'tensor'), may hold values from -0.0625 to 0.0625
- momentum: float32 [8192, 8192], P('fsdp', 'tensor'), may hold values from -700 to 700
- gradient: bfloat16 [8192, 8192], P('fsdp', 'tensor'), may hold values from -6 to 6
- probes: float32 [32, 8192], P(None, 'tensor'), may hold values from -6 to 6
Outputs:
- activations: float32 [24576, 8192], P('fsdp', 'tensor')
- momentum_out: float32 [8192, 8192], P('fsdp', 'tensor')
- krylov_scaled: float32 [96, 96], replicated
All inputs are finite; a program needn't handle non-finite values.
Results may differ from a plain program's by a relative error of at most 0.0029.
Values may be sent and summed in bfloat16 or wider, within the bound.
A program may use at most 192 MiB of HBM per device.

v0:
```python
import jax
import jax.numpy as jnp
from jax import lax
from jax.sharding import PartitionSpec as P

STEPS = 3
SQUARINGS = 5
highest = lax.Precision.HIGHEST


def hdot(left, right):
    return jnp.dot(left, right, precision=highest, preferred_element_type=jnp.float32)


def hdot_t(left, right):
    return lax.dot_general(
        left, right, (((1,), (1,)), ((), ())), precision=highest, preferred_element_type=jnp.float32
    )


def assemble(diag_blocks, low_factors):
    zero = jnp.zeros_like(diag_blocks[0])
    rows = []
    count = len(diag_blocks)
    for row in range(count):
        blocks = []
        for col in range(count):
            if row == col:
                blocks.append(diag_blocks[row])
            elif row == col + 1:
                blocks.append(low_factors[col].T)
            elif col == row + 1:
                blocks.append(low_factors[row])
            else:
                blocks.append(zero)
        rows.append(jnp.concatenate(blocks, axis=1))
    return jnp.concatenate(rows, axis=0)


def top_value(krylov):
    power = krylov / jnp.max(jnp.abs(krylov))
    for _ in range(SQUARINGS):
        power = hdot(power, power)
        power = power / jnp.max(jnp.abs(power))
    vector = jnp.sum(power, axis=1)
    vector = vector / jnp.sqrt(jnp.sum(vector * vector))
    return jnp.sum(vector * hdot(krylov, vector))


def local(tokens, weight, momentum, gradient, probes):
    moment = 0.9 * momentum + gradient.astype(jnp.float32)
    block = probes
    basis_prev = jnp.zeros_like(probes)
    diag_blocks = []
    low_factors = []
    for step in range(STEPS):
        product, gram = lax.psum((hdot_t(block, moment), hdot_t(block, block)), "tensor")
        low = jnp.linalg.cholesky(gram)
        reduced = jax.scipy.linalg.solve_triangular(low, product, lower=True)
        if step:
            low_factors.append(low)
        diag_part = hdot_t(reduced, reduced)
        if step + 1 < STEPS:
            basis = jax.scipy.linalg.solve_triangular(low, block, lower=True)
            images, diag_mat = lax.psum((hdot(reduced, moment), diag_part), "fsdp")
            residue = images - hdot(diag_mat, basis)
            if step:
                residue = residue - hdot(low.T, basis_prev)
            basis_prev, block = (basis, residue)
        else:
            diag_mat = lax.psum(diag_part, "fsdp")
        diag_blocks.append(0.5 * (diag_mat + diag_mat.T))
    krylov = assemble(diag_blocks, low_factors)
    top = top_value(krylov)
    new_weight = (weight.astype(jnp.float32) - moment / jnp.sqrt(top)).astype(jnp.bfloat16)
    summed = jnp.dot(
        tokens,
        lax.all_gather(new_weight, "fsdp", axis=0, tiled=True),
        preferred_element_type=jnp.float32,
    )
    return (summed, moment, krylov / top)


def solution(mesh):
    return jax.shard_map(
        local,
        mesh=mesh,
        in_specs=(
            P("fsdp", None),
            P("fsdp", "tensor"),
            P("fsdp", "tensor"),
            P("fsdp", "tensor"),
            P(None, "tensor"),
        ),
        out_specs=(P("fsdp", "tensor"), P("fsdp", "tensor"), P()),
        check_vma=False,
    )
```

profile of v0, /device:TPU:1, one launch (start us, length us, event | category | flops | bytes accessed | tf_op | source)
XLA Modules:
  0.0 739.3 jit_solution(580088578509843955)
XLA Ops:
  7.2 0.9 copy-done
  8.5 2.3 convert_add_fusion
  10.8 1.8 convolution_bitcast_fusion.1
  12.6 15.8 %all-reduce.2 = (f32[32,256]{0,1:T(8,128)S(1)}, f32[32,32]{0,1:T(8,128)S(1)}) all-reduce(f32[32,256]{0,1:T(8,128)S(1)} %convolution_bitcast_fusion.1, f32[32,32]{0,1:T(8,128)S(1)} %fusion.37), channel_id=1, replica_groups=mesh['fsdp'=32,'tensor'=4] {'tensor'}, use_global_device_ids=true, to_apply=%region_3.5 | all-reduce | flops 9216 | bytes 73728 | tf_op jit(solution)/shard_map/psum | solution.py:57
  28.4 2.9 cholesky.59
  32.7 2.4 custom-call.11
  35.4 2.0 fusion.39
  38.1 124.4 %psum.79 = f32[32,32]{1,0:T(8,128)S(1)} all-reduce(f32[32,32]{1,0:T(8,128)S(1)} %fusion.38), channel_id=1, replica_groups=mesh['fsdp'=32,'tensor'=4] {'fsdp'}, use_global_device_ids=true, to_apply=%region_4.7 | all-reduce | flops 1024 | bytes 8192 | tf_op jit(solution)/shard_map/psum | solution.py:65
  162.7 1.3 convolution_subtract_fusion.2
  164.3 1.9 fusion.41
  166.3 11.2 %all-reduce.1 = (f32[32,256]{1,0:T(8,128)S(1)}, f32[32,32]{0,1:T(8,128)S(1)}) all-reduce(f32[32,256]{1,0:T(8,128)S(1)} %fusion.41, f32[32,32]{0,1:T(8,128)S(1)} %fusion.40), channel_id=1, replica_groups=mesh['fsdp'=32,'tensor'=4] {'tensor'}, use_global_device_ids=true, to_apply=%region_7.0 | all-reduce | flops 9216 | bytes 73728 | tf_op jit(solution)/shard_map/psum | solution.py:57
  177.6 2.9 cholesky.70
  181.8 2.4 custom-call.13
  185.1 2.0 fusion.43
  187.2 127.2 %psum.83 = f32[32,32]{0,1:T(8,128)S(1)} all-reduce(f32[32,32]{0,1:T(8,128)S(1)} %fusion.42), channel_id=1, replica_groups=mesh['fsdp'=32,'tensor'=4] {'fsdp'}, use_global_device_ids=true, to_apply=%region_8.0 | all-reduce | flops 1024 | bytes 8192 | tf_op jit(solution)/shard_map/psum | solution.py:65
  314.8 101.5 %all-reduce.8.cloned.1.call-done = f32[32,2048]{1,0:T(8,128)} async-done(((f32[32,2048]{1,0:T(8,128)}), f32[32,2048]{1,0:T(8,128)}) %all-reduce.8.cloned.1.call-update) | async-done | bytes 262160 | tf_op jit(solution)/shard_map/psum | solution.py:65
  416.3 1.4 convolution_subtract_fusion.1
  418.4 1.9 fusion.45
  420.4 13.6 %all-reduce = (f32[32,256]{1,0:T(8,128)S(1)}, f32[32,32]{0,1:T(8,128)S(1)}) all-reduce(f32[32,256]{1,0:T(8,128)S(1)} %fusion.45, f32[32,32]{0,1:T(8,128)S(1)} %fusion.44), channel_id=1, replica_groups=mesh['fsdp'=32,'tensor'=4] {'tensor'}, use_global_device_ids=true, to_apply=%region_11.0 | all-reduce | flops 9216 | bytes 73728 | tf_op jit(solution)/shard_map/psum | solution.py:57
  434.1 2.9 cholesky.81
  438.4 2.4 custom-call.15
  441.2 122.6 %psum.87 = f32[32,32]{0,1:T(8,128)S(1)} all-reduce(f32[32,32]{0,1:T(8,128)S(1)} %fusion.46), channel_id=1, replica_groups=mesh['fsdp'=32,'tensor'=4] {'fsdp'}, use_global_device_ids=true, to_apply=%region_12.0 | all-reduce | flops 1024 | bytes 8192 | tf_op jit(solution)/shard_map/psum | solution.py:71
  564.7 1.4 abs_reduce_fusion.4
  566.1 1.4 abs_reduce_fusion.3
  567.5 1.4 abs_reduce_fusion.2
  569.0 1.4 abs_reduce_fusion.1
  570.4 1.5 abs_reduce_fusion
  575.5 1.3 subtract_convert_fusion
  576.8 1.3 broadcast_divide_fusion
  578.1 112.9 %all-gather.2.cloned.1.call-done = bf16[8192,2048]{1,0:T(8,128)(2,1)} async-done(((bf16[256,2048]{1,0:T(8,128)(2,1)}), bf16[8192,2048]{1,0:T(8,128)(2,1)}) %all-gather.2.cloned.1.call-update) | async-done | bytes 33554448 | tf_op jit(solution)/shard_map/all_gather | solution.py:78
  691.0 35.2 %convolution_bitcast_fusion = f32[768,2048]{0,1:T(8,128)} fusion(bf16[8192,2048]{1,0:T(8,128)(2,1)} %all-gather.2.cloned.1.call-done, bf16[768,8192]{1,0:T(8,128)(2,1)} %param.10), kind=kOutput, calls=%fused_computation | convolution fusion | flops 25769803776 | bytes 52428800 | tf_op jit(solution)/shard_map/dot_general | solution.py:76
  726.1 6.6 copy.38
  (54 shorter events, 11.4 us)
Async XLA Ops:
  7.2 1.0 copy-start
  7.2 155.5 %all-reduce.6.cloned.1.call-start = ((), (), s32[]{:S(2)}) async-start(), calls=%async_computation | async-start | bytes 524288 | tf_op jit(solution)/shard_map/psum | solution.py:65
  10.8 564.7 %copy-start.2 = (f32[256,2048]{1,0:T(8,128)}, f32[256,2048]{1,0:T(8,128)S(1)}, u32[]{:S(2)}) copy-start(f32[256,2048]{1,0:T(8,128)S(1)} %convert_add_fusion) | copy-start | bytes 6291460
  37.5 378.8 %all-reduce.8.cloned.1.call-start = ((), (), s32[]{:S(2)}) async-start(), calls=%async_computation.1 | async-start | bytes 524288 | tf_op jit(solution)/shard_map/psum | solution.py:65
  314.5 376.4 %all-gather.2.cloned.1.call-start = ((), (), s32[]{:S(2)}) async-start(), calls=%async_computation.2 | async-start | bytes 34603008 | tf_op jit(solution)/shard_map/all_gather | solution.py:78
  418.4 157.0 %copy-start.3 = (bf16[256,2048]{1,0:T(8,128)(2,1)S(1)}, bf16[256,2048]{1,0:T(8,128)(2,1)}, u32[]{:S(2)}) copy-start(bf16[256,2048]{1,0:T(8,128)(2,1)} %param.11) | copy-start | bytes 3145732
  726.1 6.6 copy-start.1
Sparse Core Ops, SparseCore 0:
  37.6 105.8 all-reduce.5
  314.7 101.5 all-reduce.7
  576.9 114.0 all-gather.1
where the time goes:
time: 740 us; the launch traced here: 739 us
  blocking collectives  415 us (56%)
  waiting for transfers between devices  214 us (29%)
  matrix products  59.1 us (8%)
  other arithmetic  27 us (4%)
  between operations  15.4 us (2%)
  local copies, waits for them, and re-layouts  8.1 us (1%)
    psum x2, blocking collectives, local(): images, diag_mat = lax.psum((hdot(reduced, moment), diag_part), 'fsdp')  252 us
    psum x1, blocking collectives, local(): diag_mat = lax.psum(diag_part, 'fsdp')  123 us
    all_gather x1, waiting for transfers between devices, local(): lax.all_gather(new_weight, 'fsdp', axis=0, tiled=True)  113 us
    psum x2, waiting for transfers between devices, local(): images, diag_mat = lax.psum((hdot(reduced, moment), diag_part), 'fsdp')  102 us
    psum x3, blocking collectives, local(): lax.psum((hdot_t(block, moment), hdot_t(block, block)), 'tensor')  40.7 us
    dot_general x1, matrix products, local(): jnp.dot(tokens, lax.all_gather(new_weight, 'fsdp', axis=0, tiled=True), p...  35.2 us
    dot_general x11, matrix products, hdot(): jnp.dot(left, right, precision=highest, preferred_element_type=jnp.float32)  15.2 us
  transfers between devices with their start and end apart: 3, of which 2 were waited for; matrix products, arithmetic and copies ran while one was open for 0% of the time, Pallas kernels for 0%

commit v1 on v0

--- a/solution.py
+++ b/solution.py
@@ -73,10 +73,17 @@
     krylov = assemble(diag_blocks, low_factors)
     top = top_value(krylov)
     new_weight = (weight.astype(jnp.float32) - moment / jnp.sqrt(top)).astype(jnp.bfloat16)
+
+    def build_unit_now(block_here, array_axis):
+        return jnp.concatenate(
+            lax.all_to_all(
+                jnp.stack([block_here for _ in range(lax.axis_size("fsdp"))], axis=0), "fsdp", 0, 0
+            ),
+            array_axis,
+        )
+
     summed = jnp.dot(
-        tokens,
-        lax.all_gather(new_weight, "fsdp", axis=0, tiled=True),
-        preferred_element_type=jnp.float32,
+        tokens, build_unit_now(new_weight, array_axis=0), preferred_element_type=jnp.float32
     )
     return (summed, moment, krylov / top)
 

time: 740 us -> 1190 us (1.61)
  the two profiles are of different devices: /device:TPU:1 before, /device:TPU:36 now
where the time goes in v1:
time: 1190 us
  waiting for transfers between devices  676 us (57%)
  blocking collectives  367 us (31%)
  matrix products  59.1 us (5%)
  starting transfers between devices  29.6 us (2%)
  other arithmetic  26 us (2%)
  local copies, waits for them, and re-layouts  19.1 us (2%)
  between operations  15.7 us (1%)
    all_to_all x1, waiting for transfers between devices, build_unit_now(): lax.all_to_all(jnp.stack([block_here for _ in range(lax.axis_size('fsdp')...  547 us
    psum x2, blocking collectives, local(): images, diag_mat = lax.psum((hdot(reduced, moment), diag_part), 'fsdp')  213 us
    psum x2, waiting for transfers between devices, local(): images, diag_mat = lax.psum((hdot(reduced, moment), diag_part), 'fsdp')  129 us
    psum x1, blocking collectives, local(): diag_mat = lax.psum(diag_part, 'fsdp')  101 us
    psum x3, blocking collectives, local(): lax.psum((hdot_t(block, moment), hdot_t(block, block)), 'tensor')  52.9 us
    dot_general x1, matrix products, local(): jnp.dot(tokens, build_unit_now(new_weight, array_axis=0), preferred_eleme...  35.2 us
    all_to_all x1, starting transfers between devices, build_unit_now(): lax.all_to_all(jnp.stack([block_here for _ in range(lax.axis_size('fsdp')...  29.5 us
  transfers between devices with their start and end apart: 3, of which 2 were waited for; matrix products, arithmetic and copies ran while one was open for 0% of the time, Pallas kernels for 0%

profile of v1, /device:TPU:36, one launch (start us, length us, event | category | flops | bytes accessed | tf_op | source)
XLA Modules:
  0.0 1193.0 jit_solution(522638907285204725)
XLA Ops:
  8.5 2.3 convert_add_fusion
  10.8 1.8 convolution_bitcast_fusion.1
  12.6 18.7 %all-reduce.2 = (f32[32,256]{0,1:T(8,128)S(1)}, f32[32,32]{0,1:T(8,128)S(1)}) all-reduce(f32[32,256]{0,1:T(8,128)S(1)} %convolution_bitcast_fusion.1, f32[32,32]{0,1:T(8,128)S(1)} %fusion.37), channel_id=1, replica_groups=mesh['fsdp'=32,'tensor'=4] {'tensor'}, use_global_device_ids=true, to_apply=%region_3.5 | all-reduce | flops 9216 | bytes 73728 | tf_op jit(solution)/shard_map/psum | solution.py:57
  31.4 2.9 cholesky.59
  35.6 2.4 custom-call.11
  38.4 2.0 fusion.39
  41.0 100.5 %psum.79 = f32[32,32]{1,0:T(8,128)S(1)} all-reduce(f32[32,32]{1,0:T(8,128)S(1)} %fusion.38), channel_id=1, replica_groups=mesh['fsdp'=32,'tensor'=4] {'fsdp'}, use_global_device_ids=true, to_apply=%region_4.7 | all-reduce | flops 1024 | bytes 8192 | tf_op jit(solution)/shard_map/psum | solution.py:65
  141.6 1.3 convolution_subtract_fusion.2
  143.3 1.9 fusion.41
  145.2 16.8 %all-reduce.1 = (f32[32,256]{1,0:T(8,128)S(1)}, f32[32,32]{0,1:T(8,128)S(1)}) all-reduce(f32[32,256]{1,0:T(8,128)S(1)} %fusion.41, f32[32,32]{0,1:T(8,128)S(1)} %fusion.40), channel_id=1, replica_groups=mesh['fsdp'=32,'tensor'=4] {'tensor'}, use_global_device_ids=true, to_apply=%region_7.0 | all-reduce | flops 9216 | bytes 73728 | tf_op jit(solution)/shard_map/psum | solution.py:57
  162.1 2.9 cholesky.70
  166.4 2.4 custom-call.13
  169.6 2.0 fusion.43
  171.7 112.9 %psum.83 = f32[32,32]{0,1:T(8,128)S(1)} all-reduce(f32[32,32]{0,1:T(8,128)S(1)} %fusion.42), channel_id=1, replica_groups=mesh['fsdp'=32,'tensor'=4] {'fsdp'}, use_global_device_ids=true, to_apply=%region_8.0 | all-reduce | flops 1024 | bytes 8192 | tf_op jit(solution)/shard_map/psum | solution.py:65
  284.7 129.3 %all-reduce.8.cloned.1.call-done = f32[32,2048]{1,0:T(8,128)} async-done(((f32[32,2048]{1,0:T(8,128)}), f32[32,2048]{1,0:T(8,128)}) %all-reduce.8.cloned.1.call-update) | async-done | bytes 262160 | tf_op jit(solution)/shard_map/psum | solution.py:65
  414.0 1.4 convolution_subtract_fusion.1
  416.2 1.9 fusion.45
  418.1 17.4 %all-reduce = (f32[32,256]{1,0:T(8,128)S(1)}, f32[32,32]{0,1:T(8,128)S(1)}) all-reduce(f32[32,256]{1,0:T(8,128)S(1)} %fusion.45, f32[32,32]{0,1:T(8,128)S(1)} %fusion.44), channel_id=1, replica_groups=mesh['fsdp'=32,'tensor'=4] {'tensor'}, use_global_device_ids=true, to_apply=%region_11.0 | all-reduce | flops 9216 | bytes 73728 | tf_op jit(solution)/shard_map/psum | solution.py:57
  435.6 2.9 cholesky.81
  439.9 2.4 custom-call.15
  442.7 101.2 %psum.87 = f32[32,32]{0,1:T(8,128)S(1)} all-reduce(f32[32,32]{0,1:T(8,128)S(1)} %fusion.46), channel_id=1, replica_groups=mesh['fsdp'=32,'tensor'=4] {'fsdp'}, use_global_device_ids=true, to_apply=%region_12.0 | all-reduce | flops 1024 | bytes 8192 | tf_op jit(solution)/shard_map/psum | solution.py:71
  544.8 1.4 abs_reduce_fusion.4
  546.2 1.4 abs_reduce_fusion.3
  547.7 1.4 abs_reduce_fusion.2
  549.1 1.4 abs_reduce_fusion.1
  550.5 1.5 abs_reduce_fusion
  555.9 11.0 stack.2
  566.9 29.5 %all-to-all-start = ((bf16[32,256,2048]{2,1,0:T(8,128)(2,1)}), bf16[32,256,2048]{2,1,0:T(8,128)(2,1)}, u32[]{:S(2)}, u32[]{:S(2)}) async-start(bf16[32,256,2048]{2,1,0:T(8,128)(2,1)} %stack.2), calls=%async_computation | async-start | bytes 67108864 | tf_op jit(solution)/shard_map/all_to_all | solution.py:79
  596.4 1.3 broadcast_divide_fusion
  597.7 546.7 %all-to-all-done = bf16[32,256,2048]{2,1,0:T(8,128)(2,1)} async-done(((bf16[32,256,2048]{2,1,0:T(8,128)(2,1)}), bf16[32,256,2048]{2,1,0:T(8,128)(2,1)}, u32[]{:S(2)}, u32[]{:S(2)}) %all-to-all-start) | async-done | bytes 33554464 | tf_op jit(solution)/shard_map/all_to_all | solution.py:79
  1144.4 35.2 %convolution_bitcast_fusion = f32[768,2048]{0,1:T(8,128)} fusion(bf16[8192,2048]{1,0:T(8,128)(2,1)} %bitcast.21, bf16[768,8192]{1,0:T(8,128)(2,1)} %param.10), kind=kOutput, calls=%fused_computation | convolution fusion | flops 25769803776 | bytes 52428800 | tf_op jit(solution)/shard_map/dot_general | solution.py:85
  1179.6 6.6 copy.38
  (54 shorter events, 12.3 us)
Async XLA Ops:
  7.2 1.0 copy-start
  7.2 134.4 %all-reduce.6.cloned.1.call-start = ((), (), s32[]{:S(2)}) async-start(), calls=%async_computation.1 | async-start | bytes 524288 | tf_op jit(solution)/shard_map/psum | solution.py:65
  10.8 544.7 %copy-start.2 = (f32[256,2048]{1,0:T(8,128)}, f32[256,2048]{1,0:T(8,128)S(1)}, u32[]{:S(2)}) copy-start(f32[256,2048]{1,0:T(8,128)S(1)} %convert_add_fusion) | copy-start | bytes 6291460
  40.4 373.6 %all-reduce.8.cloned.1.call-start = ((), (), s32[]{:S(2)}) async-start(), calls=%async_computation.2 | async-start | bytes 524288 | tf_op jit(solution)/shard_map/psum | solution.py:65
  416.2 139.3 %copy-start.3 = (bf16[256,2048]{1,0:T(8,128)(2,1)S(1)}, bf16[256,2048]{1,0:T(8,128)(2,1)}, u32[]{:S(2)}) copy-start(bf16[256,2048]{1,0:T(8,128)(2,1)} %param.11) | copy-start | bytes 3145732
  566.9 577.5 %all-to-all-start = ((bf16[32,256,2048]{2,1,0:T(8,128)(2,1)}), bf16[32,256,2048]{2,1,0:T(8,128)(2,1)}, u32[]{:S(2)}, u32[]{:S(2)}) async-start(bf16[32,256,2048]{2,1,0:T(8,128)(2,1)} %stack.2), calls=%async_computation | async-start | bytes 67108864 | tf_op jit(solution)/shard_map/all_to_all | solution.py:79
  1179.6 6.6 copy-start.1
Sparse Core Ops, SparseCore 0:
  40.5 100.3 all-reduce.5
  284.8 129.1 all-reduce.7
